TPU v7x, 32 devices: a whole 2x2x4 slice. The times are simulated.
32 devices in a mesh: row: 8 (over y, x, core), col: 4 (over z).
Axes of the slice: x: 2, y: 2, z: 4, core: 2. Of those that a mesh axis runs over, the one named last changes fastest.
Arguments:
- covariance: float32 [2, 8192, 8192], P(None, 'row', 'col'), as said below
- forcing: float32 [2, 8192, 8192], P(None, 'row', 'col'), as said below
- coupling: float32 [2, 64, 64], replicated, may hold values from -0.5 to 0.5
- vertical: float32 [2, 128, 128], replicated, may hold values from -0.375 to 0.375
- damping: float32 [64, 128], replicated, may hold values from 0.3 to 3
- advection: float32 [64, 128], replicated, may hold values from -2 to 2
Outputs:
- advanced: float32 [2, 8192, 8192], P(None, 'row', 'col')
Inputs may be any that keep to these rules, and one draw needn't show every extreme that they name: The covariance equals its conjugate transpose: the real plane is symmetric, the imaginary plane antisymmetric. The forcing equals its conjugate transpose: the real plane is symmetric, the imaginary plane antisymmetric.
All inputs are finite; a program needn't handle non-finite values.
Results may differ from a plain program's by a relative error of at most 0.000073.
Values sent between devices are 32-bit elements; how exact they have to be, the bound alone decides.
A program may use at most 320 MiB of HBM per device.

v0:
```python
import jax
import jax.numpy as jnp
from jax import lax
from jax.sharding import PartitionSpec as P

step_size = 0.25


def complex_einsum(pattern, factor, values):

    def single(factor_part, value_part):
        return jnp.einsum(pattern, factor_part, value_part, precision=lax.Precision.HIGHEST)

    real_part = single(factor[0], values[0]) - single(factor[1], values[1])
    imag_part = single(factor[0], values[1]) + single(factor[1], values[0])
    return jnp.stack([real_part, imag_part])


def complex_scale(factor, values):
    real_part = factor[0] * values[0] - factor[1] * values[1]
    imag_part = factor[0] * values[1] + factor[1] * values[0]
    return jnp.stack([real_part, imag_part])


def conjugate(values):
    return jnp.stack([values[0], -values[1]])


def left_apply(by_rows, coupling, vertical, rates):
    total = complex_einsum("lm,amj->alj", vertical, by_rows)
    total = total + complex_einsum("ab,blj->alj", coupling, by_rows)
    return total + complex_scale(rates[:, :, :, None], by_rows)


def right_apply(by_cols, coupling, vertical, rates):
    total = complex_einsum("lm,iam->ial", conjugate(vertical), by_cols)
    total = total + complex_einsum("ab,ibl->ial", conjugate(coupling), by_cols)
    return total + complex_scale(conjugate(rates)[:, None], by_cols)


def tendency(block_tile, forcing, coupling, vertical, rates):
    rows_here = block_tile.shape[1]
    cols_here = block_tile.shape[2]
    levels = vertical.shape[1]
    lats_row = rows_here // levels
    lats_col = cols_here // levels
    by_rows = block_tile.reshape(2, lats_row, levels, cols_here)
    regrouped = lax.all_to_all(by_rows, "row", split_axis=3, concat_axis=1, tiled=True)
    applied = left_apply(regrouped, coupling, vertical, rates)
    left_term = lax.all_to_all(applied, "row", split_axis=1, concat_axis=3, tiled=True)
    left_term = left_term.reshape(2, rows_here, cols_here)
    by_cols = block_tile.reshape(2, rows_here, lats_col, levels)
    regrouped_cols = lax.all_to_all(by_cols, "col", split_axis=1, concat_axis=2, tiled=True)
    applied_cols = right_apply(regrouped_cols, coupling, vertical, rates)
    right_term = lax.all_to_all(
        applied_cols, "col", split_axis=2, concat_axis=1, tiled=True
    ).reshape(2, rows_here, cols_here)
    return left_term + right_term + forcing


def shards(covariance, forcing, coupling, vertical, damping, advection):
    rates = jnp.stack([-damping, advection])
    first_rate = tendency(covariance, forcing, coupling, vertical, rates)
    midpoint = covariance + 0.5 * step_size * first_rate
    return covariance + step_size * tendency(midpoint, forcing, coupling, vertical, rates)


def solution(mesh):
    return jax.shard_map(
        shards,
        mesh=mesh,
        in_specs=(P(None, "row", "col"), P(None, "row", "col"), P(), P(), P(), P()),
        out_specs=P(None, "row", "col"),
        check_vma=False,
    )
```

profile of v0, /device:TPU:0, one launch (start us, length us, event | category | flops | bytes accessed | tf_op | source)
XLA Modules:
  0.0 2441.1 jit_solution(17442187832632348149)
XLA Ops:
  0.0 17.6 copy.149
  39.9 168.1 %all-to-all-done = f32[2,8,128,2048]{2,1,0,3:T(8,128)} async-done(((f32[2,8,128,2048]{2,1,0,3:T(8,128)}), f32[2,8,128,2048]{2,1,0,3:T(8,128)}, u32[]{:S(2)}, u32[]{:S(2)}) %all-to-all-start) | async-done | bytes 16777248 | tf_op jit(solution)/shard_map/all_to_all | solution.py:48
  397.3 19.0 add_bitcast_fusion.4
  439.1 137.1 %all-to-all-done.2 = f32[2,1024,16,128]{3,2,0,1:T(8,128)} async-done(((f32[2,1024,16,128]{3,2,0,1:T(8,128)}), f32[2,1024,16,128]{3,2,0,1:T(8,128)}, u32[]{:S(2)}, u32[]{:S(2)}) %all-to-all-start.2) | async-done | bytes 16777248 | tf_op jit(solution)/shard_map/all_to_all | solution.py:53
  607.0 17.1 fusion.16
  624.1 17.2 fusion.18
  641.2 17.4 fusion.20
  658.6 17.1 fusion.22
  720.1 41.0 %fusion.6 = (f32[1,256,64,128]{3,1,2,0:T(8,128)}, f32[1,256,64,128]{3,1,2,0:T(8,128)}) fusion(f32[256,128,64]{1,2,0:T(8,128)} %fusion.20, f32[256,128,64]{1,2,0:T(8,128)} %fusion.16, f32[256,128,64]{1,2,0:T(8,128)} %fusion.18, f32[256,128,64]{1,2,0:T(8,128)} %fusion.22), kind=kLoop, calls=%fused_computation.16 | loop fusion | flops 4194304 | bytes 50331648 | tf_op jit(solution)/shard_map/stack | solution.py:16
  761.2 16.7 fusion.1
  791.0 17.4 copy.164
  808.4 18.0 reshape.251
  826.3 328.4 %all-to-all-done.3 = f32[2,256,64,128]{3,1,0,2:T(8,128)} async-done(((f32[2,256,64,128]{3,1,0,2:T(8,128)}), f32[2,256,64,128]{3,1,0,2:T(8,128)}, u32[]{:S(2)}, u32[]{:S(2)}) %all-to-all-start.3) | async-done | bytes 16777248 | tf_op jit(solution)/shard_map/all_to_all | solution.py:55
  1154.7 17.8 copy.249
  1172.5 18.0 reshape.253
  1190.4 29.2 %multiply_add_fusion.1 = f32[2,1024,2048]{2,1,0:T(8,128)} fusion(f32[2,1024,2048]{2,1,0:T(8,128)} %param.6, f32[2,1024,2048]{2,1,0:T(8,128)} %param.7, f32[2,1024,2048]{2,1,0:T(8,128)} %reshape.251, f32[2,1024,2048]{2,1,0:T(8,128)} %reshape.253), kind=kLoop, calls=%fused_computation.10 | loop fusion | flops 16777216 | bytes 83886080 | tf_op jit(solution)/shard_map/add | solution.py:64
  1219.6 17.7 copy.181
  1259.5 167.4 %all-to-all-done.4 = f32[2,8,128,2048]{2,1,0,3:T(8,128)} async-done(((f32[2,8,128,2048]{2,1,0,3:T(8,128)}), f32[2,8,128,2048]{2,1,0,3:T(8,128)}, u32[]{:S(2)}, u32[]{:S(2)}) %all-to-all-start.4) | async-done | bytes 16777248 | tf_op jit(solution)/shard_map/all_to_all | solution.py:48
  1636.1 16.7 fusion.2
  1659.0 135.3 %all-to-all-done.6 = f32[2,1024,16,128]{3,2,0,1:T(8,128)} async-done(((f32[2,1024,16,128]{3,2,0,1:T(8,128)}), f32[2,1024,16,128]{3,2,0,1:T(8,128)}, u32[]{:S(2)}, u32[]{:S(2)}) %all-to-all-start.6) | async-done | bytes 16777248 | tf_op jit(solution)/shard_map/all_to_all | solution.py:53
  1828.1 17.2 fusion.14
  1845.3 17.4 fusion.12
  1862.7 17.0 fusion.10
  1879.7 17.1 fusion.8
  1934.3 18.2 fusion.5
  1952.6 18.4 fusion.4
  2012.2 17.4 copy.196
  2029.6 18.0 reshape.255
  2047.5 328.4 %all-to-all-done.7 = f32[2,256,64,128]{3,1,0,2:T(8,128)} async-done(((f32[2,256,64,128]{3,1,0,2:T(8,128)}), f32[2,256,64,128]{3,1,0,2:T(8,128)}, u32[]{:S(2)}, u32[]{:S(2)}) %all-to-all-start.7) | async-done | bytes 16777248 | tf_op jit(solution)/shard_map/all_to_all | solution.py:55
  2375.9 17.8 copy.212
  2393.7 18.0 reshape.257
  2411.7 29.2 %multiply_add_fusion = f32[2,1024,2048]{2,1,0:T(8,128)} fusion(f32[2,1024,2048]{2,1,0:T(8,128)} %param.6, f32[2,1024,2048]{2,1,0:T(8,128)} %param.7, f32[2,1024,2048]{2,1,0:T(8,128)} %reshape.255, f32[2,1024,2048]{2,1,0:T(8,128)} %reshape.257), kind=kLoop, calls=%fused_computation.9 | loop fusion | flops 16777216 | bytes 83886080 | tf_op jit(solution)/shard_map/add | solution.py:65
  (128 shorter events, 672.5 us)
Async XLA Ops:
  17.6 190.4 %all-to-all-start = ((f32[2,8,128,2048]{2,1,0,3:T(8,128)}), f32[2,8,128,2048]{2,1,0,3:T(8,128)}, u32[]{:S(2)}, u32[]{:S(2)}) async-start(f32[2,8,128,2048]{2,1,0,3:T(8,128)} %copy.149), calls=%async_computation | async-start | bytes 33554432 | tf_op jit(solution)/shard_map/all_to_all | solution.py:48
  39.9 175.3 %copy-start.13 = (f32[64,128]{1,0:T(8,128)S(1)}, f32[64,128]{1,0:T(8,128)}, u32[]{:S(2)}) copy-start(f32[64,128]{1,0:T(8,128)} %param.10) | copy-start | bytes 98308
  208.0 368.2 %all-to-all-start.2 = ((f32[2,1024,16,128]{3,2,0,1:T(8,128)}), f32[2,1024,16,128]{3,2,0,1:T(8,128)}, u32[]{:S(2)}, u32[]{:S(2)}) async-start(f32[2,1024,16,128]{3,2,0,1:T(8,128)} %copy.213), calls=%async_computation.2 | async-start | bytes 33554432 | tf_op jit(solution)/shard_map/all_to_all | solution.py:53
  215.2 497.9 %copy-start.7 = (f32[64,128]{1,0:T(8,128)}, f32[64,128]{1,0:T(8,128)S(1)}, u32[]{:S(2)}) copy-start(f32[64,128]{1,0:T(8,128)S(1)} %neg.27) | copy-start | bytes 98308
  238.7 9.2 copy-start.5
  340.0 9.3 copy-start.3
  349.3 20.4 slice-start.6
  349.3 31.2 %slice-start.4 = ((s8[8388608]{0:T(1024)(128)(4,1)}), s8[4194304]{0:T(1024)(128)(4,1)S(1)}, s32[]{:S(2)}) async-start(s8[8388608]{0:T(1024)(128)(4,1)} %bitcast.244), calls=%async_computation.12 | async-start | bytes 8388608
  360.4 9.3 slice-start.7
  360.4 20.2 slice-start.5
  380.6 9.6 copy-start.9
  576.2 207.7 %all-to-all-start.1 = ((f32[2,64,128,256]{2,3,0,1:T(8,128)}), f32[2,64,128,256]{2,3,0,1:T(8,128)}, u32[]{:S(2)}, u32[]{:S(2)}) async-start(f32[2,64,128,256]{2,3,0,1:T(8,128)} %copy.163), calls=%async_computation.1 | async-start | bytes 33554432 | tf_op jit(solution)/shard_map/all_to_all | solution.py:50
  582.2 130.9 %copy-start.11 = (f32[64,128]{1,0:T(8,128)}, f32[64,128]{1,0:T(8,128)S(1)}, u32[]{:S(2)}) copy-start(f32[64,128]{1,0:T(8,128)S(1)} %neg.32) | copy-start | bytes 98308
  784.0 370.8 %all-to-all-start.3 = ((f32[2,256,64,128]{3,1,0,2:T(8,128)}), f32[2,256,64,128]{3,1,0,2:T(8,128)}, u32[]{:S(2)}, u32[]{:S(2)}) async-start(f32[2,256,64,128]{3,1,0,2:T(8,128)} %copy.179), calls=%async_computation.3 | async-start | bytes 33554432 | tf_op jit(solution)/shard_map/all_to_all | solution.py:55
  1237.3 189.7 %all-to-all-start.4 = ((f32[2,8,128,2048]{2,1,0,3:T(8,128)}), f32[2,8,128,2048]{2,1,0,3:T(8,128)}, u32[]{:S(2)}, u32[]{:S(2)}) async-start(f32[2,8,128,2048]{2,1,0,3:T(8,128)} %copy.181), calls=%async_computation.4 | async-start | bytes 33554432 | tf_op jit(solution)/shard_map/all_to_all | solution.py:48
  1426.9 367.4 %all-to-all-start.6 = ((f32[2,1024,16,128]{3,2,0,1:T(8,128)}), f32[2,1024,16,128]{3,2,0,1:T(8,128)}, u32[]{:S(2)}, u32[]{:S(2)}) async-start(f32[2,1024,16,128]{3,2,0,1:T(8,128)} %copy.197), calls=%async_computation.6 | async-start | bytes 33554432 | tf_op jit(solution)/shard_map/all_to_all | solution.py:53
  1450.0 7.8 copy-start.2
  1461.7 9.2 copy-start.6
  1556.0 9.3 copy-start.4
  1565.3 18.7 slice-start.2
  1565.3 27.8 %slice-start = ((s8[8388608]{0:T(1024)(128)(4,1)}), s8[4194304]{0:T(1024)(128)(4,1)S(1)}, s32[]{:S(2)}) async-start(s8[8388608]{0:T(1024)(128)(4,1)} %bitcast.233), calls=%async_computation.8 | async-start | bytes 8388608
  1574.7 9.4 slice-start.3
  1574.7 18.5 slice-start.1
  1613.6 11.3 copy-start.8
  1613.6 11.3 copy-start.10
  1794.3 210.6 %all-to-all-start.5 = ((f32[2,64,128,256]{2,3,0,1:T(8,128)}), f32[2,64,128,256]{2,3,0,1:T(8,128)}, u32[]{:S(2)}, u32[]{:S(2)}) async-start(f32[2,64,128,256]{2,3,0,1:T(8,128)} %copy.195), calls=%async_computation.5 | async-start | bytes 33554432 | tf_op jit(solution)/shard_map/all_to_all | solution.py:50
  1819.1 106.0 %copy-start = (f32[1,256,4,16,128]{4,1,3,2,0:T(8,128)}, f32[1,256,4,16,128]{4,1,3,2,0:T(8,128)S(1)}, u32[]{:S(2)}) copy-start(f32[1,256,4,16,128]{4,1,3,2,0:T(8,128)S(1)} %copy.199) | copy-start | bytes 25165828
  1828.1 86.1 %copy-start.1 = (f32[1,256,4,16,128]{4,1,3,2,0:T(8,128)}, f32[1,256,4,16,128]{4,1,3,2,0:T(8,128)S(1)}, u32[]{:S(2)}) copy-start(f32[1,256,4,16,128]{4,1,3,2,0:T(8,128)S(1)} %copy.200) | copy-start | bytes 25165828
  1952.6 18.4 copy-start.12
  2004.9 371.0 %all-to-all-start.7 = ((f32[2,256,64,128]{3,1,0,2:T(8,128)}), f32[2,256,64,128]{3,1,0,2:T(8,128)}, u32[]{:S(2)}, u32[]{:S(2)}) async-start(f32[2,256,64,128]{3,1,0,2:T(8,128)} %copy.211), calls=%async_computation.7 | async-start | bytes 33554432 | tf_op jit(solution)/shard_map/all_to_all | solution.py:55
where the time goes:
time: 2450 us; the launch traced here: 2440 us
  waiting for transfers between devices  1260 us (51%)
  local copies, waits for them, and re-layouts  457 us (19%)
  matrix products  386 us (16%)
  other arithmetic  281 us (11%)
  starting transfers between devices  52 us (2%)
    all_to_all x2, waiting for transfers between devices, tendency(): lax.all_to_all(applied_cols, 'col', split_axis=2, concat_axis=1, tiled=True)  657 us
    dot_general x32, matrix products, single(): jnp.einsum(pattern, factor_part, value_part, precision=lax.Precision.HIGH...  386 us
    all_to_all x2, waiting for transfers between devices, tendency(): lax.all_to_all(by_rows, 'row', split_axis=3, concat_axis=1, tiled=True)  336 us
    all_to_all x2, waiting for transfers between devices, tendency(): lax.all_to_all(by_cols, 'col', split_axis=1, concat_axis=2, tiled=True)  272 us
    another operation x6, other arithmetic, complex_einsum(): return jnp.stack([real_part, imag_part])  119 us
    slice x12, local copies, waits for them, and re-layouts, complex_einsum(): real_part = single(factor[0], values[0]) - single(factor[1], values[1])  79.4 us
    dot_general x8, local copies, waits for them, and re-layouts, single(): jnp.einsum(pattern, factor_part, value_part, precision=lax.Precision.HIGH...  74.2 us
  transfers between devices with their start and end apart: 8, of which 6 were waited for; matrix products, arithmetic and copies ran while one was open for 39% of the time, Pallas kernels for 0%

commit v1 on v0

--- a/solution.py
+++ b/solution.py
@@ -4,6 +4,20 @@
 from jax.sharding import PartitionSpec as P
 
 step_size = 0.25
+
+
+def tell_matrix(view, along_dim, incoming_x):
+    val = view.shape
+    e_next = view.reshape(
+        *val[:along_dim], incoming_x, val[along_dim] // incoming_x, *val[along_dim + 1 :]
+    )
+    return jnp.moveaxis(e_next, along_dim, 0)
+
+
+def begin_corner(vals, d0):
+    block_now = list(vals.shape[1:])
+    block_now[d0] *= vals.shape[0]
+    return jnp.moveaxis(vals, 0, d0).reshape(block_now)
 
 
 def complex_einsum(pattern, factor, values):
@@ -50,7 +64,26 @@
     left_term = lax.all_to_all(applied, "row", split_axis=1, concat_axis=3, tiled=True)
     left_term = left_term.reshape(2, rows_here, cols_here)
     by_cols = block_tile.reshape(2, rows_here, lats_col, levels)
-    regrouped_cols = lax.all_to_all(by_cols, "col", split_axis=1, concat_axis=2, tiled=True)
+
+    def _meet_ranges(shard_in, ax_name, inputs, x_in=2):
+        p_next = lax.psum(1, axis_name=ax_name)
+        work_now = lax.axis_index(ax_name)
+        m_next, everything = (p_next, work_now)
+        response = tell_matrix(shard_in, inputs, m_next)
+        panels = [response[everything]]
+        for at in tuple(range(1, m_next)):
+            left_arr = response[(everything + at) % m_next]
+            panels.append(
+                lax.ppermute(
+                    left_arr,
+                    axis_name=ax_name,
+                    perm=[(w, (w + at) % m_next) for w in range(m_next)],
+                )
+            )
+        response = jnp.stack(panels)[(everything - jnp.arange(m_next)) % m_next]
+        return begin_corner(response, x_in)
+
+    regrouped_cols = _meet_ranges(by_cols, ax_name="col", inputs=1)
     applied_cols = right_apply(regrouped_cols, coupling, vertical, rates)
     right_term = lax.all_to_all(
         applied_cols, "col", split_axis=2, concat_axis=1, tiled=True

time: 2450 us -> 2480 us (1.012)
  waiting for transfers between devices: 1260 us -> 1070 us
  starting transfers between devices: 52 us -> 219 us
  local copies, waits for them, and re-layouts: 457 us -> 497 us
  other arithmetic: 281 us -> 306 us
    ppermute x0 -> x6, waiting for transfers between devices: none -> 489 us  [_meet_ranges(): lax.ppermute(left_arr, axis_name=ax_name, perm=[(w, (w + at) % m_next) fo...]
    all_to_all x2, waiting for transfers between devices: 657 us -> 280 us  [tendency(): lax.all_to_all(applied_cols, 'col', split_axis=2, concat_axis=1, tiled=True)]
    all_to_all x2, waiting for transfers between devices: 336 us -> 0.01 us  [tendency(): lax.all_to_all(by_rows, 'row', split_axis=3, concat_axis=1, tiled=True)]
    all_to_all x2, waiting for transfers between devices: 0.01 us -> 297 us  [tendency(): lax.all_to_all(applied, 'row', split_axis=1, concat_axis=3, tiled=True)]
    all_to_all x2 -> x0, waiting for transfers between devices: 272 us -> none  [tendency(): lax.all_to_all(by_cols, 'col', split_axis=1, concat_axis=2, tiled=True)]
    all_to_all x2, starting transfers between devices: 14.3 us -> 184 us  [tendency(): lax.all_to_all(applied_cols, 'col', split_axis=2, concat_axis=1, tiled=True)]
    gather x0 -> x6, local copies, waits for them, and re-layouts: none -> 44.1 us  [_meet_ranges(): response = jnp.stack(panels)[(everything - jnp.arange(m_next)) % m_next]]
  transfers between devices with their start and end apart: 8 -> 12, of which waited for: 6 -> 8; matrix products, arithmetic and copies ran while one was open for 39% -> 41% of each run, Pallas kernels for 0% -> 0%
where the time goes in v1:
time: 2480 us
  waiting for transfers between devices  1070 us (43%)
  local copies, waits for them, and re-layouts  497 us (20%)
  matrix products  386 us (16%)
  other arithmetic  306 us (12%)
  starting transfers between devices  219 us (9%)
    ppermute x6, waiting for transfers between devices, _meet_ranges(): lax.ppermute(left_arr, axis_name=ax_name, perm=[(w, (w + at) % m_next) fo...  489 us
    dot_general x32, matrix products, single(): jnp.einsum(pattern, factor_part, value_part, precision=lax.Precision.HIGH...  386 us
    all_to_all x2, waiting for transfers between devices, tendency(): lax.all_to_all(applied, 'row', split_axis=1, concat_axis=3, tiled=True)  297 us
    all_to_all x2, waiting for transfers between devices, tendency(): lax.all_to_all(applied_cols, 'col', split_axis=2, concat_axis=1, tiled=True)  280 us
    all_to_all x2, starting transfers between devices, tendency(): lax.all_to_all(applied_cols, 'col', split_axis=2, concat_axis=1, tiled=True)  184 us
    another operation x6, other arithmetic, complex_einsum(): return jnp.stack([real_part, imag_part])  119 us
    slice x12, local copies, waits for them, and re-layouts, complex_einsum(): real_part = single(factor[0], values[0]) - single(factor[1], values[1])  79.6 us
    dot_general x8, local copies, waits for them, and re-layouts, single(): jnp.einsum(pattern, factor_part, value_part, precision=lax.Precision.HIGH...  74.2 us
  transfers between devices with their start and end apart: 12, of which 8 were waited for; matrix products, arithmetic and copies ran while one was open for 41% of the time, Pallas kernels for 0%

profile of v1, /device:TPU:0, one launch (start us, length us, event | category | flops | bytes accessed | tf_op | source)
XLA Modules:
  0.0 2475.2 jit_solution(8303265567410762608)
XLA Ops:
  33.3 17.6 copy.165
  57.1 66.2 %collective-permute-done = f32[2,256,16,128]{3,2,1,0:T(8,128)} collective-permute-done((f32[2,256,16,128]{3,2,1,0:T(8,128)}, f32[2,256,16,128]{3,2,1,0:T(8,128)}, u32[]{:S(2)}, u32[]{:S(2)}) %collective-permute-start) | collective-permute-done | bytes 4194336 | tf_op jit(solution)/shard_map/ppermute | solution.py:77
  123.3 178.9 %collective-permute-done.1 = f32[2,256,16,128]{3,2,1,0:T(8,128)} collective-permute-done((f32[2,256,16,128]{3,2,1,0:T(8,128)}, f32[2,256,16,128]{3,2,1,0:T(8,128)}, u32[]{:S(2)}, u32[]{:S(2)}) %collective-permute-start.1) | collective-permute-done | bytes 4194336 | tf_op jit(solution)/shard_map/ppermute | solution.py:77
  355.2 17.1 fusion.16
  372.3 17.1 fusion.18
  389.4 17.4 fusion.20
  468.5 40.8 %fusion.6 = (f32[1,256,64,128]{3,1,2,0:T(8,128)}, f32[1,256,64,128]{3,1,2,0:T(8,128)}) fusion(f32[256,128,64]{1,2,0:T(8,128)} %fusion.20, f32[256,128,64]{1,2,0:T(8,128)} %fusion.16, f32[256,128,64]{1,2,0:T(8,128)} %fusion.18, f32[256,128,64]{1,2,0:T(8,128)} %fusion.22), kind=kLoop, calls=%fused_computation.24 | loop fusion | flops 4194304 | bytes 50331648 | tf_op jit(solution)/shard_map/stack | solution.py:30
  532.1 92.6 %all-to-all-start.2 = ((f32[2,256,64,128]{3,1,0,2:T(8,128)}), f32[2,256,64,128]{3,1,0,2:T(8,128)}, u32[]{:S(2)}, u32[]{:S(2)}) async-start(f32[2,256,64,128]{3,1,0,2:T(8,128)} %copy.197), calls=%async_computation.2 | async-start | bytes 33554432 | tf_op jit(solution)/shard_map/all_to_all | solution.py:88
  806.6 18.9 add_bitcast_fusion.4
  848.5 140.7 %all-to-all-done.2 = f32[2,256,64,128]{3,1,0,2:T(8,128)} async-done(((f32[2,256,64,128]{3,1,0,2:T(8,128)}), f32[2,256,64,128]{3,1,0,2:T(8,128)}, u32[]{:S(2)}, u32[]{:S(2)}) %all-to-all-start.2) | async-done | bytes 16777248 | tf_op jit(solution)/shard_map/all_to_all | solution.py:88
  995.3 17.7 copy.276
  1013.1 18.0 reshape.311
  1031.0 148.2 %all-to-all-done.1 = f32[2,64,128,256]{2,3,0,1:T(8,128)} async-done(((f32[2,64,128,256]{2,3,0,1:T(8,128)}), f32[2,64,128,256]{2,3,0,1:T(8,128)}, u32[]{:S(2)}, u32[]{:S(2)}) %all-to-all-start.1) | async-done | bytes 16777248 | tf_op jit(solution)/shard_map/all_to_all | solution.py:64
  1179.3 17.4 copy.180
  1196.6 18.0 reshape.310
  1214.6 29.2 %multiply_add_fusion.1 = f32[2,1024,2048]{2,1,0:T(8,128)} fusion(f32[2,1024,2048]{2,1,0:T(8,128)} %param.6, f32[2,1024,2048]{2,1,0:T(8,128)} %param.7, f32[2,1024,2048]{2,1,0:T(8,128)} %reshape.310, f32[2,1024,2048]{2,1,0:T(8,128)} %reshape.311), kind=kLoop, calls=%fused_computation.18 | loop fusion | flops 16777216 | bytes 83886080 | tf_op jit(solution)/shard_map/add | solution.py:97
  1263.0 17.7 copy.199
  1286.6 68.1 %collective-permute-done.3 = f32[2,256,16,128]{3,2,1,0:T(8,128)} collective-permute-done((f32[2,256,16,128]{3,2,1,0:T(8,128)}, f32[2,256,16,128]{3,2,1,0:T(8,128)}, u32[]{:S(2)}, u32[]{:S(2)}) %collective-permute-start.3) | collective-permute-done | bytes 4194336 | tf_op jit(solution)/shard_map/ppermute | solution.py:77
  1354.7 175.7 %collective-permute-done.4 = f32[2,256,16,128]{3,2,1,0:T(8,128)} collective-permute-done((f32[2,256,16,128]{3,2,1,0:T(8,128)}, f32[2,256,16,128]{3,2,1,0:T(8,128)}, u32[]{:S(2)}, u32[]{:S(2)}) %collective-permute-start.4) | collective-permute-done | bytes 4194336 | tf_op jit(solution)/shard_map/ppermute | solution.py:77
  1587.1 17.2 fusion.14
  1604.3 17.1 fusion.12
  1621.4 17.3 fusion.10
  1693.5 18.2 fusion.5
  1711.7 18.4 fusion.4
  1764.0 91.8 %all-to-all-start.5 = ((f32[2,256,64,128]{3,1,0,2:T(8,128)}), f32[2,256,64,128]{3,1,0,2:T(8,128)}, u32[]{:S(2)}, u32[]{:S(2)}) async-start(f32[2,256,64,128]{3,1,0,2:T(8,128)} %copy.231), calls=%async_computation.5 | async-start | bytes 33554432 | tf_op jit(solution)/shard_map/all_to_all | solution.py:88
  2080.9 138.8 %all-to-all-done.5 = f32[2,256,64,128]{3,1,0,2:T(8,128)} async-done(((f32[2,256,64,128]{3,1,0,2:T(8,128)}), f32[2,256,64,128]{3,1,0,2:T(8,128)}, u32[]{:S(2)}, u32[]{:S(2)}) %all-to-all-start.5) | async-done | bytes 16777248 | tf_op jit(solution)/shard_map/all_to_all | solution.py:88
  2225.8 17.7 copy.232
  2243.5 18.0 reshape.314
  2261.4 149.0 %all-to-all-done.4 = f32[2,64,128,256]{2,3,0,1:T(8,128)} async-done(((f32[2,64,128,256]{2,3,0,1:T(8,128)}), f32[2,64,128,256]{2,3,0,1:T(8,128)}, u32[]{:S(2)}, u32[]{:S(2)}) %all-to-all-start.4) | async-done | bytes 16777248 | tf_op jit(solution)/shard_map/all_to_all | solution.py:64
  2410.4 17.4 copy.214
  2427.8 18.0 reshape.313
  2445.8 29.2 %multiply_add_fusion = f32[2,1024,2048]{2,1,0:T(8,128)} fusion(f32[2,1024,2048]{2,1,0:T(8,128)} %param.6, f32[2,1024,2048]{2,1,0:T(8,128)} %param.7, f32[2,1024,2048]{2,1,0:T(8,128)} %reshape.313, f32[2,1024,2048]{2,1,0:T(8,128)} %reshape.314), kind=kLoop, calls=%fused_computation.17 | loop fusion | flops 16777216 | bytes 83886080 | tf_op jit(solution)/shard_map/add | solution.py:98
  (154 shorter events, 789.0 us)
Async XLA Ops:
  26.3 97.0 %collective-permute-start = (f32[2,256,16,128]{3,2,1,0:T(8,128)}, f32[2,256,16,128]{3,2,1,0:T(8,128)}, u32[]{:S(2)}, u32[]{:S(2)}) collective-permute-start(f32[2,256,16,128]{3,2,1,0:T(8,128)} %get-tuple-element.29), channel_id=1, source_target_pairs={{0,1},{1,2},{2,3},{3,0},{4,5},{5,6},{6,7},{7,4},{8,9},{9,10},{10,1... | collective-permute-start | bytes 12582920 | tf_op jit(solution)/shard_map/ppermute | solution.py:77
  29.4 272.8 %collective-permute-start.1 = (f32[2,256,16,128]{3,2,1,0:T(8,128)}, f32[2,256,16,128]{3,2,1,0:T(8,128)}, u32[]{:S(2)}, u32[]{:S(2)}) collective-permute-start(f32[2,256,16,128]{3,2,1,0:T(8,128)} %get-tuple-element.28), channel_id=1, source_target_pairs={{0,2},{1,3},{2,0},{3,1},{4,6},{5,7},{6,4},{7,5},{8,10},{9,11},{10,... | collective-permute-start | bytes 12582920 | tf_op jit(solution)/shard_map/ppermute | solution.py:77
  32.0 270.2 %collective-permute-start.2 = (f32[2,256,16,128]{3,2,1,0:T(8,128)}, f32[2,256,16,128]{3,2,1,0:T(8,128)}, u32[]{:S(2)}, u32[]{:S(2)}) collective-permute-start(f32[2,256,16,128]{3,2,1,0:T(8,128)} %get-tuple-element.30), channel_id=1, source_target_pairs={{0,3},{1,0},{2,1},{3,2},{4,7},{5,4},{6,5},{7,6},{8,11},{9,8},{10,9... | collective-permute-start | bytes 12582920 | tf_op jit(solution)/shard_map/ppermute | solution.py:77
  51.0 481.1 %all-to-all-start = ((f32[2,8,128,2048]{2,1,0,3:T(8,128)}), f32[2,8,128,2048]{2,1,0,3:T(8,128)}, u32[]{:S(2)}, u32[]{:S(2)}) async-start(f32[2,8,128,2048]{2,1,0,3:T(8,128)} %copy.165), calls=%async_computation | async-start | bytes 33554432 | tf_op jit(solution)/shard_map/all_to_all | solution.py:62
  57.1 404.3 %copy-start.7 = (f32[64,128]{1,0:T(8,128)}, f32[64,128]{1,0:T(8,128)S(1)}, u32[]{:S(2)}) copy-start(f32[64,128]{1,0:T(8,128)S(1)} %neg.27) | copy-start | bytes 98308
  57.1 404.3 %copy-start.14 = (f32[64,128]{1,0:T(8,128)}, f32[64,128]{1,0:T(8,128)S(1)}, u32[]{:S(2)}) copy-start(f32[64,128]{1,0:T(8,128)S(1)} %neg.32) | copy-start | bytes 98308
  57.1 265.6 %copy-start.17 = (s32[1024]{0:T(1024)}, s32[1024]{0:T(1024)S(1)}, u32[]{:S(2)}) copy-start(s32[1024]{0:T(1024)S(1)} %pad_clamp_fusion) | copy-start | bytes 12292
  406.8 17.0 copy-start.3
  532.1 457.1 %all-to-all-start.2 = ((f32[2,256,64,128]{3,1,0,2:T(8,128)}), f32[2,256,64,128]{3,1,0,2:T(8,128)}, u32[]{:S(2)}, u32[]{:S(2)}) async-start(f32[2,256,64,128]{3,1,0,2:T(8,128)} %copy.197), calls=%async_computation.2 | async-start | bytes 33554432 | tf_op jit(solution)/shard_map/all_to_all | solution.py:88
  759.1 20.3 slice-start.6
  759.1 31.2 %slice-start.4 = ((s8[8388608]{0:T(1024)(128)(4,1)}), s8[4194304]{0:T(1024)(128)(4,1)S(1)}, s32[]{:S(2)}) async-start(s8[8388608]{0:T(1024)(128)(4,1)} %bitcast.282), calls=%async_computation.10 | async-start | bytes 8388608
  770.1 20.2 slice-start.5
  790.3 9.4 copy-start.8
  790.3 9.4 copy-start.12
  989.2 190.1 %all-to-all-start.1 = ((f32[2,64,128,256]{2,3,0,1:T(8,128)}), f32[2,64,128,256]{2,3,0,1:T(8,128)}, u32[]{:S(2)}, u32[]{:S(2)}) async-start(f32[2,64,128,256]{2,3,0,1:T(8,128)} %copy.179), calls=%async_computation.1 | async-start | bytes 33554432 | tf_op jit(solution)/shard_map/all_to_all | solution.py:64
  1259.1 95.6 %collective-permute-start.3 = (f32[2,256,16,128]{3,2,1,0:T(8,128)}, f32[2,256,16,128]{3,2,1,0:T(8,128)}, u32[]{:S(2)}, u32[]{:S(2)}) collective-permute-start(f32[2,256,16,128]{3,2,1,0:T(8,128)} %get-tuple-element.19), channel_id=1, source_target_pairs={{0,1},{1,2},{2,3},{3,0},{4,5},{5,6},{6,7},{7,4},{8,9},{9,10},{10,1... | collective-permute-start | bytes 12582920 | tf_op jit(solution)/shard_map/ppermute | solution.py:77
  1259.6 270.9 %collective-permute-start.4 = (f32[2,256,16,128]{3,2,1,0:T(8,128)}, f32[2,256,16,128]{3,2,1,0:T(8,128)}, u32[]{:S(2)}, u32[]{:S(2)}) collective-permute-start(f32[2,256,16,128]{3,2,1,0:T(8,128)} %get-tuple-element.18), channel_id=1, source_target_pairs={{0,2},{1,3},{2,0},{3,1},{4,6},{5,7},{6,4},{7,5},{8,10},{9,11},{10,... | collective-permute-start | bytes 12582920 | tf_op jit(solution)/shard_map/ppermute | solution.py:77
  1263.0 267.5 %collective-permute-start.5 = (f32[2,256,16,128]{3,2,1,0:T(8,128)}, f32[2,256,16,128]{3,2,1,0:T(8,128)}, u32[]{:S(2)}, u32[]{:S(2)}) collective-permute-start(f32[2,256,16,128]{3,2,1,0:T(8,128)} %get-tuple-element.20), channel_id=1, source_target_pairs={{0,3},{1,0},{2,1},{3,2},{4,7},{5,4},{6,5},{7,6},{8,11},{9,8},{10,9... | collective-permute-start | bytes 12582920 | tf_op jit(solution)/shard_map/ppermute | solution.py:77
  1280.7 483.3 %all-to-all-start.3 = ((f32[2,8,128,2048]{2,1,0,3:T(8,128)}), f32[2,8,128,2048]{2,1,0,3:T(8,128)}, u32[]{:S(2)}, u32[]{:S(2)}) async-start(f32[2,8,128,2048]{2,1,0,3:T(8,128)} %copy.199), calls=%async_computation.3 | async-start | bytes 33554432 | tf_op jit(solution)/shard_map/all_to_all | solution.py:62
  1578.1 105.9 %copy-start = (f32[1,256,4,16,128]{4,1,3,2,0:T(8,128)}, f32[1,256,4,16,128]{4,1,3,2,0:T(8,128)S(1)}, u32[]{:S(2)}) copy-start(f32[1,256,4,16,128]{4,1,3,2,0:T(8,128)S(1)} %copy.219) | copy-start | bytes 25165828
  1587.1 86.0 %copy-start.1 = (f32[1,256,4,16,128]{4,1,3,2,0:T(8,128)}, f32[1,256,4,16,128]{4,1,3,2,0:T(8,128)S(1)}, u32[]{:S(2)}) copy-start(f32[1,256,4,16,128]{4,1,3,2,0:T(8,128)S(1)} %copy.220) | copy-start | bytes 25165828
  1638.8 17.1 copy-start.4
  1711.7 18.4 copy-start.9
  1711.7 18.4 copy-start.15
  1764.0 455.8 %all-to-all-start.5 = ((f32[2,256,64,128]{3,1,0,2:T(8,128)}), f32[2,256,64,128]{3,1,0,2:T(8,128)}, u32[]{:S(2)}, u32[]{:S(2)}) async-start(f32[2,256,64,128]{3,1,0,2:T(8,128)} %copy.231), calls=%async_computation.5 | async-start | bytes 33554432 | tf_op jit(solution)/shard_map/all_to_all | solution.py:88
  1987.2 18.7 slice-start.2
  1987.2 27.8 %slice-start = ((s8[8388608]{0:T(1024)(128)(4,1)}), s8[4194304]{0:T(1024)(128)(4,1)S(1)}, s32[]{:S(2)}) async-start(s8[8388608]{0:T(1024)(128)(4,1)} %bitcast.271), calls=%async_computation.6 | async-start | bytes 8388608
  1996.5 9.4 slice-start.3
  1996.5 18.5 slice-start.1
  2035.5 11.3 copy-start.10
  2035.5 11.3 copy-start.13
  2219.7 190.7 %all-to-all-start.4 = ((f32[2,64,128,256]{2,3,0,1:T(8,128)}), f32[2,64,128,256]{2,3,0,1:T(8,128)}, u32[]{:S(2)}, u32[]{:S(2)}) async-start(f32[2,64,128,256]{2,3,0,1:T(8,128)} %copy.213), calls=%async_computation.4 | async-start | bytes 33554432 | tf_op jit(solution)/shard_map/all_to_all | solution.py:64
  (6 other events, 44.3 us)
